TPU v7x, 32 devices: a whole 2x2x4 slice. The times are simulated.
32 devices in a mesh: img: 4 (over x, core), cls: 4 (over z), tpl: 2 (over y).
Axes of the slice: x: 2, y: 2, z: 4, core: 2. Of those that a mesh axis runs over, the one named last changes fastest.
Arguments:
- images: bfloat16 [2048, 1280], P(('img', 'tpl')), may hold values from -5 to 5
- labels: int32 [2048], P(('img', 'tpl')), may hold values from 0 to 1023
- templates: bfloat16 [8, 1024, 1280], P('tpl', ('cls', 'img')), may hold values from -0.125 to 0.125
- projection: bfloat16 [1280, 1280], P('img', 'cls'), may hold values from -0.08441157 to 0.08441157
Outputs:
- grad_templates: bfloat16 [8, 1024, 1280], P('tpl', ('cls', 'img'))
- grad_projection: float32 [1280, 1280], P('img', 'cls')
All inputs are finite; a program needn't handle non-finite values.
Results may differ from a plain program's by a relative error of at most 0.011.
Values may be sent and summed in bfloat16 or wider, within the bound.
No kernel may reach another device: no remote copies, remote signals or barrier semaphores. Data moves between devices by JAX's collectives and lax.ppermute only.
A program may use at most 64 MiB of HBM per device.

v0:
```python
import jax
import jax.numpy as jnp
from jax import lax
from jax.sharding import PartitionSpec as P

logit_scale = 50.0
epsilon = 1e-06


def inverse_norm(values):
    return lax.rsqrt(jnp.sum(values * values, axis=-1, keepdims=True) + epsilon)


def body(images, labels, templates, projection):
    tpl_count = templates.shape[0]
    cls_count = templates.shape[1]
    feat_width = templates.shape[2]
    tpl_total = tpl_count * lax.axis_size("tpl")
    img_count = lax.axis_size("img")
    wide_proj = lax.all_gather(projection, "cls", axis=1, tiled=True)
    full_proj = lax.all_gather(wide_proj, "img", axis=0, tiled=True)
    flat_tpl = templates.reshape(tpl_count * cls_count, feat_width)
    text_z = jnp.dot(flat_tpl, full_proj, preferred_element_type=jnp.float32)
    text_rz = inverse_norm(text_z)
    text_u = text_z * text_rz
    u_three = text_u.reshape(tpl_count, cls_count, feat_width)
    local_sum = jnp.sum(u_three, axis=0)
    mean_emb = lax.psum(local_sum, "tpl") / tpl_total
    mean_rn = inverse_norm(mean_emb)
    class_w = mean_emb * mean_rn
    class_b = class_w.astype(jnp.bfloat16)
    img_f = images.astype(jnp.float32)
    img_b = (img_f * inverse_norm(img_f)).astype(jnp.bfloat16)
    class_panel = lax.all_gather(class_b, "img", axis=0, tiled=True)
    scores = logit_scale * jnp.einsum(
        "cd,nd->cn", class_panel, img_b, preferred_element_type=jnp.float32
    )
    exp_scores = jnp.exp(scores)
    totals = lax.psum(jnp.sum(exp_scores, axis=0), "cls")
    first_id = lax.axis_index("cls") * img_count * cls_count
    class_ids = first_id + lax.broadcasted_iota(jnp.int32, (class_panel.shape[0], 1), 0)
    one_hot = (labels[None, :] == class_ids).astype(jnp.float32)
    grad_logit = (exp_scores / totals[None, :] - one_hot).astype(jnp.bfloat16)
    spread = lax.psum_scatter(
        logit_scale * jnp.dot(grad_logit, img_b, preferred_element_type=jnp.float32),
        "img",
        scatter_dimension=0,
        tiled=True,
    )
    class_g = lax.psum(spread, "tpl")
    dot_wg = jnp.sum(class_w * class_g, axis=1, keepdims=True)
    grad_mean = (class_g - class_w * dot_wg) * mean_rn
    per_u = grad_mean / tpl_total
    inner_prod = jnp.sum(u_three * per_u[None], axis=2, keepdims=True)
    grad_z = (
        (per_u[None] - u_three * inner_prod) * text_rz.reshape(tpl_count, cls_count, 1)
    ).astype(jnp.bfloat16)
    grad_flat = grad_z.reshape(tpl_count * cls_count, feat_width)
    grad_tpl = lax.dot_general(
        grad_flat, full_proj, (((1,), (1,)), ((), ())), preferred_element_type=jnp.float32
    )
    grad_templates = grad_tpl.astype(jnp.bfloat16).reshape(tpl_count, cls_count, feat_width)
    tpl_columns = lax.all_to_all(flat_tpl, "img", split_axis=1, concat_axis=0, tiled=True)
    partial_proj = lax.dot_general(
        tpl_columns,
        lax.all_gather(grad_flat, "img", axis=0, tiled=True),
        (((0,), (0,)), ((), ())),
        preferred_element_type=jnp.float32,
    )
    shared_proj = lax.psum_scatter(
        partial_proj.astype(jnp.bfloat16), "cls", scatter_dimension=1, tiled=True
    )
    grad_projection = lax.psum(shared_proj, "tpl").astype(jnp.float32)
    return (grad_templates, grad_projection)


def solution(mesh):
    in_specs = (
        P(("img", "tpl"), None),
        P(("img", "tpl")),
        P("tpl", ("cls", "img"), None),
        P("img", "cls"),
    )
    out_specs = (P("tpl", ("cls", "img"), None), P("img", "cls"))
    return jax.shard_map(body, mesh=mesh, in_specs=in_specs, out_specs=out_specs, check_vma=False)
```

profile of v0, /device:TPU:0, one launch (start us, length us, event | category | flops | bytes accessed | tf_op | source)
XLA Modules:
  0.0 261.0 jit_solution(5731900698816479913)
XLA Ops:
  7.2 1.1 copy.10
  8.3 23.5 %all_gather.12 = bf16[320,1280]{0,1:T(8,128)(2,1)S(1)} all-gather(bf16[320,320]{0,1:T(8,128)(2,1)S(1)} %copy.10), channel_id=1, replica_groups=mesh['img'=4,'cls'=4,'tpl'=2] {'cls'}, dimensions={1}, use_global_device_ids=true | all-gather | bytes 1024000 | tf_op jit(solution)/shard_map/all_gather | solution.py:20
  31.8 1.3 copy.11
  33.2 0.2 fusion.1
  33.4 29.0 %all-gather.3.cloned.1.call-done = bf16[1280,1280]{1,0:T(8,128)(2,1)} async-done(((bf16[320,1280]{1,0:T(8,128)(2,1)}), bf16[1280,1280]{1,0:T(8,128)(2,1)}) %all-gather.3.cloned.1.call-update) | async-done | bytes 3276816 | tf_op jit(solution)/shard_map/all_gather | solution.py:21
  62.4 3.0 %multiply_reduce_fusion = (f32[256]{0:T(256)S(1)}, f32[256,1280]{1,0:T(8,128)S(1)}) fusion(bf16[256,1280]{1,0:T(8,128)(2,1)S(1)} %bitcast.29, bf16[1280,1280]{1,0:T(8,128)(2,1)} %all-gather.3.cloned.1.call-done), kind=kOutput, calls=%fused_computation.13 | convolution fusion | flops 839515904 | bytes 5243904 | tf_op jit(solution)/shard_map/dot_general | solution.py:23
  65.5 0.2 broadcast_multiply_fusion
  65.7 0.8 reduce_sum.64
  66.6 24.4 %all-reduce.4.cloned.1.call-done = f32[64,1280]{1,0:T(8,128)} async-done(((f32[64,1280]{1,0:T(8,128)}), f32[64,1280]{1,0:T(8,128)}) %all-reduce.4.cloned.1.call-update) | async-done | bytes 327696 | tf_op jit(solution)/shard_map/psum | solution.py:28
  91.0 1.1 multiply_reduce_fusion.2
  92.1 1.1 multiply_convert_fusion
  93.2 7.9 %all_gather.14 = bf16[256,1280]{1,0:T(8,128)(2,1)S(1)} all-gather(bf16[64,1280]{1,0:T(8,128)(2,1)S(1)} %multiply_convert_fusion), channel_id=1, replica_groups=mesh['img'=4,'cls'=4,'tpl'=2] {'img'}, dimensions={0}, use_global_device_ids=true | all-gather | bytes 819200 | tf_op jit(solution)/shard_map/all_gather | solution.py:34
  101.1 0.5 fusion.12
  101.5 11.7 %psum.29 = f32[256]{0:T(256)S(1)} all-reduce(f32[256]{0:T(256)S(1)} %get-tuple-element.6), channel_id=1, replica_groups=mesh['img'=4,'cls'=4,'tpl'=2] {'cls'}, use_global_device_ids=true, to_apply=%region_6.0 | all-reduce | flops 256 | bytes 2048 | tf_op jit(solution)/shard_map/psum | solution.py:39
  113.2 1.5 convolution_multiply_fusion
  114.8 23.3 %reduce-scatter.5.cloned.1.call-done = f32[64,1280]{1,0:T(8,128)} async-done(((f32[256,1280]{1,0:T(8,128)}), f32[64,1280]{1,0:T(8,128)}) %reduce-scatter.5.cloned.1.call-update) | async-done | bytes 327696 | tf_op jit(solution)/shard_map/reduce_scatter | solution.py:44
  138.2 26.4 %all-reduce.6.cloned.1.call-done = f32[64,1280]{1,0:T(8,128)} async-done(((f32[64,1280]{1,0:T(8,128)}), f32[64,1280]{1,0:T(8,128)}) %all-reduce.6.cloned.1.call-update) | async-done | bytes 327696 | tf_op jit(solution)/shard_map/psum | solution.py:50
  164.6 1.2 multiply_reduce_fusion.1
  165.8 1.1 multiply_multiply_fusion
  166.9 0.3 fusion.3
  167.2 1.1 fusion.5
  168.4 0.9 all_to_all.14
  169.3 0.6 copy.12
  169.9 17.5 %all_to_all.19 = bf16[256,4,320]{0,2,1:T(8,128)(2,1)S(1)} all-to-all(bf16[256,4,320]{0,2,1:T(8,128)(2,1)S(1)} %copy.12), channel_id=1, replica_groups=mesh['img'=4,'cls'=4,'tpl'=2] {'img'}, dimensions={1} | all-to-all | bytes 1310720 | tf_op jit(solution)/shard_map/all_to_all | solution.py:63
  187.5 10.8 %all-gather.5.cloned.1.call-done = bf16[1024,1280]{1,0:T(8,128)(2,1)} async-done(((bf16[256,1280]{1,0:T(8,128)(2,1)}), bf16[1024,1280]{1,0:T(8,128)(2,1)}) %all-gather.5.cloned.1.call-update) | async-done | bytes 2621456 | tf_op jit(solution)/shard_map/all_gather | solution.py:66
  198.3 2.7 %fusion = bf16[320,1280]{1,0:T(8,128)(2,1)S(1)} fusion(bf16[1024,320]{0,1:T(8,128)(2,1)S(1)} %bitcast.30, bf16[1024,1280]{1,0:T(8,128)(2,1)} %all-gather.5.cloned.1.call-done), kind=kOutput, calls=%fused_computation.3 | convolution fusion | flops 839270400 | bytes 4096000 | tf_op jit(solution)/shard_map/dot_general | solution.py:64
  201.0 1.3 copy.14
  202.4 25.5 %reduce-scatter.7.cloned.1.call-done = bf16[320,320]{1,0:T(8,128)(2,1)} async-done(((bf16[1280,320]{1,0:T(8,128)(2,1)}), bf16[320,320]{1,0:T(8,128)(2,1)}) %reduce-scatter.7.cloned.1.call-update) | async-done | bytes 204816
  227.9 1.8 copy.15
  229.7 3.8 %convolution_convert_fusion.1 = bf16[256,1280]{1,0:T(8,128)(2,1)} fusion(bf16[256,1280]{1,0:T(8,128)(2,1)S(1)} %copy-done.1, bf16[1280,1280]{1,0:T(8,128)(2,1)} %all-gather.3.cloned.1.call-done), kind=kOutput, calls=%fused_computation.2 | convolution fusion | flops 839188480 | bytes 4587520 | tf_op jit(solution)/shard_map/dot_general | solution.py:59
  233.5 18.9 %all-reduce.8.cloned.1.call-done = bf16[320,320]{1,0:T(8,128)(2,1)} async-done(((bf16[320,320]{1,0:T(8,128)(2,1)}), bf16[320,320]{1,0:T(8,128)(2,1)}) %all-reduce.8.cloned.1.call-update) | async-done | bytes 204816 | tf_op jit(solution)/shard_map/psum | solution.py:73
  252.4 1.8 convert_element_type.40
  (31 shorter events, 0.5 us)
Async XLA Ops:
  7.2 55.3 %all-gather.3.cloned.1.call-start = ((), (), s32[]{:S(2)}) async-start(), calls=%async_computation.3 | async-start | bytes 4096000 | tf_op jit(solution)/shard_map/all_gather | solution.py:21
  31.8 1.4 copy-start.2
  31.8 30.6 %copy-start.3 = (bf16[4,64,1280]{2,1,0:T(8,128)(2,1)S(1)}, bf16[4,64,1280]{2,1,0:T(8,128)(2,1)}, u32[]{:S(2)}) copy-start(bf16[4,64,1280]{2,1,0:T(8,128)(2,1)} %param.6) | copy-start | bytes 1966084
  33.1 57.9 %all-reduce.4.cloned.1.call-start = ((), (), s32[]{:S(2)}) async-start(), calls=%async_computation.4 | async-start | bytes 655360 | tf_op jit(solution)/shard_map/psum | solution.py:28
  66.5 71.6 %reduce-scatter.5.cloned.1.call-start = ((), (), s32[]{:S(2)}) async-start(), calls=%async_computation.5 | async-start | bytes 1638400 | tf_op jit(solution)/shard_map/reduce_scatter | solution.py:44
  93.2 20.1 %copy-start.5 = (s32[256]{0:T(256)S(1)}, s32[256]{0:T(256)}, u32[]{:S(2)}) copy-start(s32[256]{0:T(256)} %param.5) | copy-start | bytes 3076
  114.7 49.9 %copy-start = (f32[64,1280]{1,0:T(8,128)S(1)}, f32[64,1280]{1,0:T(8,128)}, u32[]{:S(2)}) copy-start(f32[64,1280]{1,0:T(8,128)} %all-reduce.4.cloned.1.call-done) | copy-start | bytes 983044
  114.8 49.8 %all-reduce.6.cloned.1.call-start = ((), (), s32[]{:S(2)}) async-start(), calls=%async_computation.6 | async-start | bytes 655360 | tf_op jit(solution)/shard_map/psum | solution.py:50
  138.1 60.2 %all-gather.5.cloned.1.call-start = ((), (), s32[]{:S(2)}) async-start(), calls=%async_computation.7 | async-start | bytes 3276800 | tf_op jit(solution)/shard_map/all_gather | solution.py:66
  167.2 1.2 copy-start.4
  168.4 59.5 %reduce-scatter.7.cloned.1.call-start = ((), (), s32[]{:S(2)}) async-start(), calls=%async_computation.9 | async-start | bytes 1228800
  202.3 27.4 %copy-start.1 = (bf16[256,1280]{1,0:T(8,128)(2,1)S(1)}, bf16[256,1280]{1,0:T(8,128)(2,1)}, u32[]{:S(2)}) copy-start(bf16[256,1280]{1,0:T(8,128)(2,1)} %fusion.5) | copy-start | bytes 1966084
  202.4 50.0 %all-reduce.8.cloned.1.call-start = ((), (), s32[]{:S(2)}) async-start(), calls=%async_computation.8 | async-start | bytes 491520 | tf_op jit(solution)/shard_map/psum | solution.py:73
Sparse Core Ops, SparseCore 0:
  33.2 29.1 all-gather.2
  66.6 24.3 all-reduce.3
  114.9 23.1 reduce-scatter.4
  140.2 24.3 all-reduce.5
  168.5 29.7 all-gather.4
  202.5 25.3 reduce-scatter.6
  230.7 21.6 all-reduce.7
where the time goes:
time: 262 us; the launch traced here: 261 us
  waiting for transfers between devices  158 us (60%)
  blocking collectives  60.5 us (23%)
  between operations  14.3 us (5%)
  matrix products  11.6 us (4%)
  other arithmetic  8.86 us (3%)
  local copies, waits for them, and re-layouts  7.09 us (3%)
    all_gather x1, waiting for transfers between devices, body(): full_proj = lax.all_gather(wide_proj, 'img', axis=0, tiled=True)  29 us
    psum x1, waiting for transfers between devices, body(): class_g = lax.psum(spread, 'tpl')  26.4 us
    unnamed x8, waiting for transfers between devices  25.6 us
    psum x1, waiting for transfers between devices, body(): mean_emb = lax.psum(local_sum, 'tpl') / tpl_total  24.4 us
    all_gather x1, blocking collectives, body(): wide_proj = lax.all_gather(projection, 'cls', axis=1, tiled=True)  23.5 us
    reduce_scatter x1, waiting for transfers between devices, body(): lax.psum_scatter(logit_scale * jnp.dot(grad_logit, img_b, preferred_eleme...  23.3 us
    psum x1, waiting for transfers between devices, body(): grad_projection = lax.psum(shared_proj, 'tpl').astype(jnp.float32)  18.9 us
    all_to_all x1, blocking collectives, body(): lax.all_to_all(flat_tpl, 'img', split_axis=1, concat_axis=0, tiled=True)  17.5 us
  transfers between devices with their start and end apart: 7, of which 7 were waited for; matrix products, arithmetic and copies ran while one was open for 2% of the time, Pallas kernels for 0%

commit v1 on v0

--- a/solution.py
+++ b/solution.py
@@ -5,6 +5,11 @@
 
 logit_scale = 50.0
 epsilon = 1e-06
+
+
+def summed_here(x, axis):
+    parts = lax.all_gather(x, axis)
+    return jnp.sum(parts, axis=0)
 
 
 def inverse_norm(values):
@@ -25,7 +30,7 @@
     text_u = text_z * text_rz
     u_three = text_u.reshape(tpl_count, cls_count, feat_width)
     local_sum = jnp.sum(u_three, axis=0)
-    mean_emb = lax.psum(local_sum, "tpl") / tpl_total
+    mean_emb = summed_here(local_sum, "tpl") / tpl_total
     mean_rn = inverse_norm(mean_emb)
     class_w = mean_emb * mean_rn
     class_b = class_w.astype(jnp.bfloat16)

time: 262 us -> 245 us (0.935)
  waiting for transfers between devices: 158 us -> 135 us
  blocking collectives: 60.5 us -> 70.2 us
  other arithmetic: 8.86 us -> 6.23 us
    psum x1 -> x0, waiting for transfers between devices: 24.4 us -> none  [body(): mean_emb = lax.psum(local_sum, 'tpl') / tpl_total]
    all_gather x0 -> x1, blocking collectives: none -> 10.5 us  [summed_here(): parts = lax.all_gather(x, axis)]
    unnamed x8 -> x7, waiting for transfers between devices: 25.6 us -> 25.6 us
  transfers between devices with their start and end apart: 7 -> 6, of which waited for: 7 -> 6; matrix products, arithmetic and copies ran while one was open for 2% -> 2% of each run, Pallas kernels for 0% -> 0%
where the time goes in v1:
time: 245 us
  waiting for transfers between devices  135 us (55%)
  blocking collectives  70.2 us (29%)
  between operations  14.2 us (6%)
  matrix products  11.6 us (5%)
  local copies, waits for them, and re-layouts  7.09 us (3%)
  other arithmetic  6.23 us (3%)
    all_gather x1, waiting for transfers between devices, body(): full_proj = lax.all_gather(wide_proj, 'img', axis=0, tiled=True)  29 us
    psum x1, waiting for transfers between devices, body(): class_g = lax.psum(spread, 'tpl')  26.6 us
    unnamed x7, waiting for transfers between devices  25.6 us
    reduce_scatter x1, waiting for transfers between devices, body(): lax.psum_scatter(logit_scale * jnp.dot(grad_logit, img_b, preferred_eleme...  24.6 us
    all_gather x1, blocking collectives, body(): wide_proj = lax.all_gather(projection, 'cls', axis=1, tiled=True)  23.5 us
    psum x1, waiting for transfers between devices, body(): grad_projection = lax.psum(shared_proj, 'tpl').astype(jnp.float32)  18.7 us
    all_to_all x1, blocking collectives, body(): lax.all_to_all(flat_tpl, 'img', split_axis=1, concat_axis=0, tiled=True)  17.5 us
    psum x1, blocking collectives, body(): totals = lax.psum(jnp.sum(exp_scores, axis=0), 'cls')  11.7 us
  transfers between devices with their start and end apart: 6, of which 6 were waited for; matrix products, arithmetic and copies ran while one was open for 2% of the time, Pallas kernels for 0%

profile of v1, /device:TPU:0, one launch (start us, length us, event | category | flops | bytes accessed | tf_op | source)
XLA Modules:
  0.0 244.8 jit_solution(15652575733572654541)
XLA Ops:
  7.2 1.1 copy.14
  8.3 23.5 %all_gather.18 = bf16[320,1280]{0,1:T(8,128)(2,1)S(1)} all-gather(bf16[320,320]{0,1:T(8,128)(2,1)S(1)} %copy.14), channel_id=1, replica_groups=mesh['img'=4,'cls'=4,'tpl'=2] {'cls'}, dimensions={1}, use_global_device_ids=true | all-gather | bytes 1024000 | tf_op jit(solution)/shard_map/all_gather | solution.py:25
  31.8 1.3 copy.15
  33.2 0.2 fusion.1
  33.4 29.0 %all-gather.4.cloned.1.call-done = bf16[1280,1280]{1,0:T(8,128)(2,1)} async-done(((bf16[320,1280]{1,0:T(8,128)(2,1)}), bf16[1280,1280]{1,0:T(8,128)(2,1)}) %all-gather.4.cloned.1.call-update) | async-done | bytes 3276816 | tf_op jit(solution)/shard_map/all_gather | solution.py:26
  62.4 3.0 %multiply_reduce_fusion = (f32[256]{0:T(256)S(1)}, f32[256,1280]{1,0:T(8,128)S(1)}) fusion(bf16[256,1280]{1,0:T(8,128)(2,1)S(1)} %bitcast.31, bf16[1280,1280]{1,0:T(8,128)(2,1)} %all-gather.4.cloned.1.call-done), kind=kOutput, calls=%fused_computation.13 | convolution fusion | flops 839515904 | bytes 5243904 | tf_op jit(solution)/shard_map/dot_general | solution.py:28
  65.5 0.2 broadcast_multiply_fusion
  65.7 0.1 reduce_sum.73
  65.8 10.5 %all-gather = f32[128,1280]{1,0:T(8,128)S(1)} all-gather(f32[64,1280]{1,0:T(8,128)S(1)} %reduce_sum.73), channel_id=2, replica_groups=mesh['img'=4,'cls'=4,'tpl'=2] {'tpl'}, dimensions={0}, use_global_device_ids=true | all-gather | bytes 983040 | tf_op jit(solution)/shard_map/all_gather | solution.py:11
  76.3 0.1 multiply_reduce_fusion.2
  76.5 0.1 multiply_convert_fusion
  76.6 7.0 %all_gather.22 = bf16[256,1280]{1,0:T(8,128)(2,1)S(1)} all-gather(bf16[64,1280]{1,0:T(8,128)(2,1)S(1)} %multiply_convert_fusion), channel_id=1, replica_groups=mesh['img'=4,'cls'=4,'tpl'=2] {'img'}, dimensions={0}, use_global_device_ids=true | all-gather | bytes 819200 | tf_op jit(solution)/shard_map/all_gather | solution.py:39
  83.6 0.5 fusion.12
  84.1 11.7 %psum.21 = f32[256]{0:T(256)S(1)} all-reduce(f32[256]{0:T(256)S(1)} %get-tuple-element.6), channel_id=1, replica_groups=mesh['img'=4,'cls'=4,'tpl'=2] {'cls'}, use_global_device_ids=true, to_apply=%region_6.0 | all-reduce | flops 256 | bytes 2048 | tf_op jit(solution)/shard_map/psum | solution.py:44
  95.8 1.5 convolution_multiply_fusion
  97.3 24.6 %reduce-scatter.5.cloned.1.call-done = f32[64,1280]{1,0:T(8,128)} async-done(((f32[256,1280]{1,0:T(8,128)}), f32[64,1280]{1,0:T(8,128)}) %reduce-scatter.5.cloned.1.call-update) | async-done | bytes 327696 | tf_op jit(solution)/shard_map/reduce_scatter | solution.py:49
  122.0 26.6 %all-reduce.3.cloned.1.call-done = f32[64,1280]{1,0:T(8,128)} async-done(((f32[64,1280]{1,0:T(8,128)}), f32[64,1280]{1,0:T(8,128)}) %all-reduce.3.cloned.1.call-update) | async-done | bytes 327696 | tf_op jit(solution)/shard_map/psum | solution.py:55
  148.6 1.2 multiply_reduce_fusion.1
  149.8 1.1 multiply_multiply_fusion
  150.9 0.3 fusion.3
  151.2 1.1 fusion.5
  152.4 0.9 all_to_all.14
  153.3 0.6 copy.16
  153.9 17.5 %all_to_all.19 = bf16[256,4,320]{0,2,1:T(8,128)(2,1)S(1)} all-to-all(bf16[256,4,320]{0,2,1:T(8,128)(2,1)S(1)} %copy.16), channel_id=1, replica_groups=mesh['img'=4,'cls'=4,'tpl'=2] {'img'}, dimensions={1} | all-to-all | bytes 1310720 | tf_op jit(solution)/shard_map/all_to_all | solution.py:68
  171.5 10.8 %all-gather.6.cloned.1.call-done = bf16[1024,1280]{1,0:T(8,128)(2,1)} async-done(((bf16[256,1280]{1,0:T(8,128)(2,1)}), bf16[1024,1280]{1,0:T(8,128)(2,1)}) %all-gather.6.cloned.1.call-update) | async-done | bytes 2621456 | tf_op jit(solution)/shard_map/all_gather | solution.py:71
  182.3 2.7 %fusion = bf16[320,1280]{1,0:T(8,128)(2,1)S(1)} fusion(bf16[1024,320]{0,1:T(8,128)(2,1)S(1)} %bitcast.32, bf16[1024,1280]{1,0:T(8,128)(2,1)} %all-gather.6.cloned.1.call-done), kind=kOutput, calls=%fused_computation.3 | convolution fusion | flops 839270400 | bytes 4096000 | tf_op jit(solution)/shard_map/dot_general | solution.py:69
  185.0 1.3 copy.18
  186.4 25.5 %reduce-scatter.7.cloned.1.call-done = bf16[320,320]{1,0:T(8,128)(2,1)} async-done(((bf16[1280,320]{1,0:T(8,128)(2,1)}), bf16[320,320]{1,0:T(8,128)(2,1)}) %reduce-scatter.7.cloned.1.call-update) | async-done | bytes 204816
  211.9 1.8 copy.19
  213.7 3.8 %convolution_convert_fusion.1 = bf16[256,1280]{1,0:T(8,128)(2,1)} fusion(bf16[256,1280]{1,0:T(8,128)(2,1)S(1)} %copy-done, bf16[1280,1280]{1,0:T(8,128)(2,1)} %all-gather.4.cloned.1.call-done), kind=kOutput, calls=%fused_computation.2 | convolution fusion | flops 839188480 | bytes 4587520 | tf_op jit(solution)/shard_map/dot_general | solution.py:64
  217.5 18.7 %all-reduce.5.cloned.1.call-done = bf16[320,320]{1,0:T(8,128)(2,1)} async-done(((bf16[320,320]{1,0:T(8,128)(2,1)}), bf16[320,320]{1,0:T(8,128)(2,1)}) %all-reduce.5.cloned.1.call-update) | async-done | bytes 204816 | tf_op jit(solution)/shard_map/psum | solution.py:78
  236.2 1.8 convert_element_type.40
  (30 shorter events, 0.5 us)
Async XLA Ops:
  7.2 55.3 %all-gather.4.cloned.1.call-start = ((), (), s32[]{:S(2)}) async-start(), calls=%async_computation.3 | async-start | bytes 4096000 | tf_op jit(solution)/shard_map/all_gather | solution.py:26
  31.8 1.4 copy-start.1
  31.8 30.6 %copy-start.3 = (bf16[4,64,1280]{2,1,0:T(8,128)(2,1)S(1)}, bf16[4,64,1280]{2,1,0:T(8,128)(2,1)}, u32[]{:S(2)}) copy-start(bf16[4,64,1280]{2,1,0:T(8,128)(2,1)} %param.6) | copy-start | bytes 1966084
  33.1 88.8 %reduce-scatter.5.cloned.1.call-start = ((), (), s32[]{:S(2)}) async-start(), calls=%async_computation.4 | async-start | bytes 1638400 | tf_op jit(solution)/shard_map/reduce_scatter | solution.py:49
  76.3 7.3 %copy-start.2 = (bf16[256,1280]{1,0:T(8,128)(2,1)S(1)}, bf16[256,1280]{1,0:T(8,128)(2,1)}, u32[]{:S(2)}) copy-start(bf16[256,1280]{1,0:T(8,128)(2,1)} %param.4) | copy-start | bytes 1966084
  76.6 19.2 %copy-start.5 = (s32[256]{0:T(256)S(1)}, s32[256]{0:T(256)}, u32[]{:S(2)}) copy-start(s32[256]{0:T(256)} %param.5) | copy-start | bytes 3076
  97.3 51.3 %all-reduce.3.cloned.1.call-start = ((), (), s32[]{:S(2)}) async-start(), calls=%async_computation.5 | async-start | bytes 655360 | tf_op jit(solution)/shard_map/psum | solution.py:55
  121.9 60.3 %all-gather.6.cloned.1.call-start = ((), (), s32[]{:S(2)}) async-start(), calls=%async_computation.6 | async-start | bytes 3276800 | tf_op jit(solution)/shard_map/all_gather | solution.py:71
  151.2 1.2 copy-start.4
  152.3 59.5 %reduce-scatter.7.cloned.1.call-start = ((), (), s32[]{:S(2)}) async-start(), calls=%async_computation.8 | async-start | bytes 1228800
  186.3 27.4 %copy-start = (bf16[256,1280]{1,0:T(8,128)(2,1)S(1)}, bf16[256,1280]{1,0:T(8,128)(2,1)}, u32[]{:S(2)}) copy-start(bf16[256,1280]{1,0:T(8,128)(2,1)} %fusion.5) | copy-start | bytes 1966084
  186.3 49.9 %all-reduce.5.cloned.1.call-start = ((), (), s32[]{:S(2)}) async-start(), calls=%async_computation.7 | async-start | bytes 491520 | tf_op jit(solution)/shard_map/psum | solution.py:78
Sparse Core Ops, SparseCore 0:
  33.2 29.1 all-gather.3
  97.4 24.4 reduce-scatter.4
  124.2 24.3 all-reduce.2
  152.5 29.7 all-gather.5
  186.5 25.3 reduce-scatter.6
  214.6 21.6 all-reduce.4
